TPU v7x, 256 devices: a whole 4x4x8 slice. The times are simulated.
256 devices in a mesh: dp: 16 (over z, x_hi), pipe: 4 (over y), tensor: 4 (over x_lo, core).
Axes of the slice: x: 4 (x_hi: 2, x_lo: 2; x = x_hi * 2 + x_lo), y: 4, z: 8, core: 2. Of those that a mesh axis runs over, the one named last changes fastest.
Arguments:
- grad_out: bfloat16 [8, 1024, 4096], P(None, 'dp', 'tensor'), may hold values from -6 to 6
- activations: bfloat16 [4, 3, 8, 1024, 4096], P('pipe', None, None, 'dp', 'tensor'), may hold values from -6 to 6
- mixing: bfloat16 [4, 3, 32, 128, 128], P('pipe', None, 'tensor'), may hold values from -0.1875 to 0.1875
- proj_tiles: bfloat16 [4, 3, 8, 128, 128], P('pipe'), may hold values from -0.1875 to 0.1875
- proj_blocks: int32 [4, 3, 8], P('pipe'), may hold values from 0 to 31, all different within a row
- section_sizes: int32 [4], replicated, may hold values from 1 to 3, 8 in all
Outputs:
- segment_grads: bfloat16 [4, 8, 1024, 4096], P('pipe', None, 'dp', 'tensor')
- sketches: float32 [4, 3, 8, 4096], P('pipe')
Inputs may be any that keep to these rules, and one draw needn't show every extreme that they name: `section_sizes`: each segment holds 1 to 3 layers, 8 in all, some segment exactly 3. `proj_blocks`: the 8 blocks of one slot are distinct.
All inputs are finite; a program needn't handle non-finite values.
Results may differ from a plain program's by a relative error of at most 0.0074.
Values may be sent and summed in bfloat16 or wider, within the bound.
A program may use at most 64 MiB of HBM per device.

v0:
```python
import math
import jax
import jax.numpy as jnp
from jax import lax
from jax.sharding import PartitionSpec as P


def shifted(x, axis, by):
    peers = lax.axis_size(axis)
    pairs = [(i, i + by) for i in range(peers) if 0 <= i + by < peers]
    return lax.ppermute(x, axis, pairs)


def silu_slope(value):
    sig = jax.nn.sigmoid(value)
    return sig * (1.0 + value * (1.0 - sig))


def shards(grad_out, activations, mixing, proj_tiles, proj_blocks, section_sizes):
    high = lax.Precision.HIGHEST
    segments = lax.axis_size("pipe")
    segment = lax.axis_index("pipe")
    half = lax.axis_index("tensor")
    micro = grad_out.shape[0]
    tokens = grad_out.shape[1]
    local_width = grad_out.shape[2]
    slots = activations.shape[1]
    heads_local = mixing.shape[2]
    head_size = mixing.shape[3]
    rank = proj_tiles.shape[4] // 2
    scale = 1.0 / math.sqrt(tokens * lax.axis_size("dp"))
    live_count = section_sizes[segment]
    owned = heads_local * half + jnp.arange(heads_local, dtype=jnp.int32)
    select = (proj_blocks[0][:, :, None] == owned[None, None, :]).astype(jnp.bfloat16)
    dense = jnp.einsum("kjb,kjcr->kbcr", select, proj_tiles[0], preferred_element_type=jnp.float32)
    dense = dense.astype(jnp.bfloat16).reshape(slots, heads_local * head_size, 2 * rank)
    live_slots = jnp.arange(slots, dtype=jnp.int32) < live_count

    def process(grad, start, width):
        acts = lax.dynamic_slice_in_dim(activations[0], start, width, 1)
        act_parts = [None] * slots
        delta_parts = [None] * slots
        for slot in range(slots - 1, -1, -1):
            flat_act = acts[slot].reshape(width * tokens, local_width)
            heads_in = acts[slot].reshape(width, tokens, heads_local, head_size)
            pre = jnp.einsum(
                "mthc,hcd->mthd", heads_in, mixing[0, slot], preferred_element_type=jnp.float32
            )
            grad_heads = grad.reshape(width, tokens, heads_local, head_size).astype(jnp.float32)
            delta = (grad_heads * silu_slope(pre)).astype(jnp.bfloat16)
            back = jnp.einsum(
                "mthd,hcd->mthc", delta, mixing[0, slot], preferred_element_type=jnp.float32
            )
            moved = (grad_heads + back).reshape(width, tokens, local_width).astype(jnp.bfloat16)
            grad = jnp.where(slot < live_count, moved, grad)
            act_parts[slot] = jnp.dot(
                flat_act, dense[slot, :, :rank], preferred_element_type=jnp.float32
            )
            delta_parts[slot] = jnp.dot(
                delta.reshape(width * tokens, local_width),
                dense[slot, :, rank:],
                preferred_element_type=jnp.float32,
            )
        act_proj, grad_proj = lax.psum((jnp.stack(act_parts), jnp.stack(delta_parts)), "tensor")
        act_proj = act_proj.reshape(slots, width, tokens, rank)
        grad_proj = grad_proj.reshape(slots, width, tokens, rank)
        sketch = jnp.einsum("kmtr,kmts->kmrs", grad_proj, act_proj, precision=high) * scale
        sketch = jnp.where(live_slots[:, None, None, None], sketch, 0.0).reshape(
            slots, width, rank * rank
        )
        return (grad, sketch)

    width = 1
    groups = micro // width
    turns = groups + segments - 1

    def turn(step, carry):
        incoming, segment_out, sketches = carry
        group = step - (segments - 1 - segment)
        valid = jnp.logical_and(group >= 0, group < groups)
        start = jnp.clip(group, 0, groups - 1) * width
        top = lax.dynamic_slice_in_dim(grad_out, start, width, 0)
        grad = jnp.where(segment == segments - 1, top, incoming)
        grad, sketch = process(grad, start, width)
        sketch = lax.psum(sketch, "dp")
        old_out = lax.dynamic_slice_in_dim(segment_out, start, width, 0)
        segment_out = lax.dynamic_update_slice_in_dim(
            segment_out, jnp.where(valid, grad, old_out), start, 0
        )
        old_sketch = lax.dynamic_slice_in_dim(sketches, start, width, 1)
        sketches = lax.dynamic_update_slice_in_dim(
            sketches, jnp.where(valid, sketch, old_sketch), start, 1
        )
        incoming = shifted(grad, "pipe", -1)
        return (incoming, segment_out, sketches)

    start_carry = (
        jnp.zeros((width, tokens, local_width), jnp.bfloat16),
        jnp.zeros_like(grad_out),
        jnp.zeros((slots, micro, rank * rank), jnp.float32),
    )
    incoming, segment_out, sketches = lax.fori_loop(0, turns, turn, start_carry)
    return (segment_out[None], sketches[None])


def solution(mesh):
    return jax.shard_map(
        shards,
        mesh=mesh,
        in_specs=(
            P(None, "dp", "tensor"),
            P("pipe", None, None, "dp", "tensor"),
            P("pipe", None, "tensor", None, None),
            P("pipe", None, None, None, None),
            P("pipe", None, None),
            P(),
        ),
        out_specs=(P("pipe", None, "dp", "tensor"), P("pipe", None, None, None)),
        check_vma=False,
    )
```

profile of v0, /device:TPU:8, one launch (start us, length us, event | category | flops | bytes accessed | tf_op | source)
XLA Modules:
  0.0 1463.1 jit_solution(14424018004752751403)
XLA Ops:
  7.2 1.4 dynamic_slice.35
  13.3 1442.5 %while.20 = (s32[]{:T(128)}, bf16[1,64,1024]{2,1,0:T(8,128)(2,1)S(1)}, bf16[8,64,1024]{2,1,0:T(8,128)(2,1)}, f32[3,8,4096]{2,1,0:T(8,128)S(1)}, pred[]{:T(512)},...) while((s32[]{:T(128)}, ...), condition=%wide.region_4.5_spmd.clone, body=%wide.region_0.4_spmd.clone.sunk | while | flops 163307520 | bytes 16024470 | solution.py:102
  17.3 1.6 select_dynamic-update-slice_fusion.2
  19.0 4.1 collective-permute-start
  29.5 41.9 %all-reduce.5.cloned.1.call-done = (f32[3,64,64]{2,1,0:T(8,128)}, f32[3,64,64]{2,1,0:T(8,128)}) async-done(((f32[3,64,64]{2,1,0:T(8,128)}, f32[3,64,64]{2,1,0:T(8,128)}), (f32[3,64,64]{2,1,0:T(8,128)}, f32[3,64,64]{2,1,0:T(8,128)})) %all-reduce.5.cloned.1.call-update) | async-done | bytes 98320 | tf_op jit(solution)/shard_map/while/body/eval_jaxpr/psum | solution.py:64
  72.8 77.3 %psum.43 = f32[3,1,4096]{2,0,1:T(4,128)S(1)} all-reduce(f32[3,1,4096]{2,0,1:T(4,128)S(1)} %reshape.292), channel_id=1, replica_groups=mesh['dp'=16,'pipe'=4,'tensor'=4] {'dp'}, use_global_device_ids=true, to_apply=%region_3.3 | all-reduce | flops 12288 | bytes 98304 | tf_op jit(solution)/shard_map/while/body/eval_jaxpr/psum | solution.py:85
  154.6 1.6 select_dynamic-update-slice_fusion.2
  156.3 2.4 collective-permute-start
  165.2 36.7 %all-reduce.5.cloned.1.call-done = (f32[3,64,64]{2,1,0:T(8,128)}, f32[3,64,64]{2,1,0:T(8,128)}) async-done(((f32[3,64,64]{2,1,0:T(8,128)}, f32[3,64,64]{2,1,0:T(8,128)}), (f32[3,64,64]{2,1,0:T(8,128)}, f32[3,64,64]{2,1,0:T(8,128)})) %all-reduce.5.cloned.1.call-update) | async-done | bytes 98320 | tf_op jit(solution)/shard_map/while/body/eval_jaxpr/psum | solution.py:64
  203.3 77.3 %psum.43 = f32[3,1,4096]{2,0,1:T(4,128)S(1)} all-reduce(f32[3,1,4096]{2,0,1:T(4,128)S(1)} %reshape.292), channel_id=1, replica_groups=mesh['dp'=16,'pipe'=4,'tensor'=4] {'dp'}, use_global_device_ids=true, to_apply=%region_3.3 | all-reduce | flops 12288 | bytes 98304 | tf_op jit(solution)/shard_map/while/body/eval_jaxpr/psum | solution.py:85
  285.2 1.6 select_dynamic-update-slice_fusion.2
  286.8 2.4 collective-permute-start
  295.7 36.7 %all-reduce.5.cloned.1.call-done = (f32[3,64,64]{2,1,0:T(8,128)}, f32[3,64,64]{2,1,0:T(8,128)}) async-done(((f32[3,64,64]{2,1,0:T(8,128)}, f32[3,64,64]{2,1,0:T(8,128)}), (f32[3,64,64]{2,1,0:T(8,128)}, f32[3,64,64]{2,1,0:T(8,128)})) %all-reduce.5.cloned.1.call-update) | async-done | bytes 98320 | tf_op jit(solution)/shard_map/while/body/eval_jaxpr/psum | solution.py:64
  332.4 1.3 fusion.129
  333.8 77.3 %psum.43 = f32[3,1,4096]{2,0,1:T(4,128)S(1)} all-reduce(f32[3,1,4096]{2,0,1:T(4,128)S(1)} %reshape.292), channel_id=1, replica_groups=mesh['dp'=16,'pipe'=4,'tensor'=4] {'dp'}, use_global_device_ids=true, to_apply=%region_3.3 | all-reduce | flops 12288 | bytes 98304 | tf_op jit(solution)/shard_map/while/body/eval_jaxpr/psum | solution.py:85
  415.7 1.6 select_dynamic-update-slice_fusion.2
  417.3 2.4 collective-permute-start
  426.2 36.7 %all-reduce.5.cloned.1.call-done = (f32[3,64,64]{2,1,0:T(8,128)}, f32[3,64,64]{2,1,0:T(8,128)}) async-done(((f32[3,64,64]{2,1,0:T(8,128)}, f32[3,64,64]{2,1,0:T(8,128)}), (f32[3,64,64]{2,1,0:T(8,128)}, f32[3,64,64]{2,1,0:T(8,128)})) %all-reduce.5.cloned.1.call-update) | async-done | bytes 98320 | tf_op jit(solution)/shard_map/while/body/eval_jaxpr/psum | solution.py:64
  462.9 1.3 fusion.129
  464.3 77.3 %psum.43 = f32[3,1,4096]{2,0,1:T(4,128)S(1)} all-reduce(f32[3,1,4096]{2,0,1:T(4,128)S(1)} %reshape.292), channel_id=1, replica_groups=mesh['dp'=16,'pipe'=4,'tensor'=4] {'dp'}, use_global_device_ids=true, to_apply=%region_3.3 | all-reduce | flops 12288 | bytes 98304 | tf_op jit(solution)/shard_map/while/body/eval_jaxpr/psum | solution.py:85
  546.2 1.6 select_dynamic-update-slice_fusion.2
  547.8 2.4 collective-permute-start
  556.8 36.7 %all-reduce.5.cloned.1.call-done = (f32[3,64,64]{2,1,0:T(8,128)}, f32[3,64,64]{2,1,0:T(8,128)}) async-done(((f32[3,64,64]{2,1,0:T(8,128)}, f32[3,64,64]{2,1,0:T(8,128)}), (f32[3,64,64]{2,1,0:T(8,128)}, f32[3,64,64]{2,1,0:T(8,128)})) %all-reduce.5.cloned.1.call-update) | async-done | bytes 98320 | tf_op jit(solution)/shard_map/while/body/eval_jaxpr/psum | solution.py:64
  594.9 77.3 %psum.43 = f32[3,1,4096]{2,0,1:T(4,128)S(1)} all-reduce(f32[3,1,4096]{2,0,1:T(4,128)S(1)} %reshape.292), channel_id=1, replica_groups=mesh['dp'=16,'pipe'=4,'tensor'=4] {'dp'}, use_global_device_ids=true, to_apply=%region_3.3 | all-reduce | flops 12288 | bytes 98304 | tf_op jit(solution)/shard_map/while/body/eval_jaxpr/psum | solution.py:85
  676.7 1.6 select_dynamic-update-slice_fusion.2
  678.4 2.4 collective-permute-start
  687.3 36.7 %all-reduce.5.cloned.1.call-done = (f32[3,64,64]{2,1,0:T(8,128)}, f32[3,64,64]{2,1,0:T(8,128)}) async-done(((f32[3,64,64]{2,1,0:T(8,128)}, f32[3,64,64]{2,1,0:T(8,128)}), (f32[3,64,64]{2,1,0:T(8,128)}, f32[3,64,64]{2,1,0:T(8,128)})) %all-reduce.5.cloned.1.call-update) | async-done | bytes 98320 | tf_op jit(solution)/shard_map/while/body/eval_jaxpr/psum | solution.py:64
  725.4 77.3 %psum.43 = f32[3,1,4096]{2,0,1:T(4,128)S(1)} all-reduce(f32[3,1,4096]{2,0,1:T(4,128)S(1)} %reshape.292), channel_id=1, replica_groups=mesh['dp'=16,'pipe'=4,'tensor'=4] {'dp'}, use_global_device_ids=true, to_apply=%region_3.3 | all-reduce | flops 12288 | bytes 98304 | tf_op jit(solution)/shard_map/while/body/eval_jaxpr/psum | solution.py:85
  807.3 1.6 select_dynamic-update-slice_fusion.2
  808.9 2.4 collective-permute-start
  817.8 36.7 %all-reduce.5.cloned.1.call-done = (f32[3,64,64]{2,1,0:T(8,128)}, f32[3,64,64]{2,1,0:T(8,128)}) async-done(((f32[3,64,64]{2,1,0:T(8,128)}, f32[3,64,64]{2,1,0:T(8,128)}), (f32[3,64,64]{2,1,0:T(8,128)}, f32[3,64,64]{2,1,0:T(8,128)})) %all-reduce.5.cloned.1.call-update) | async-done | bytes 98320 | tf_op jit(solution)/shard_map/while/body/eval_jaxpr/psum | solution.py:64
  855.9 77.3 %psum.43 = f32[3,1,4096]{2,0,1:T(4,128)S(1)} all-reduce(f32[3,1,4096]{2,0,1:T(4,128)S(1)} %reshape.292), channel_id=1, replica_groups=mesh['dp'=16,'pipe'=4,'tensor'=4] {'dp'}, use_global_device_ids=true, to_apply=%region_3.3 | all-reduce | flops 12288 | bytes 98304 | tf_op jit(solution)/shard_map/while/body/eval_jaxpr/psum | solution.py:85
  937.8 1.6 select_dynamic-update-slice_fusion.2
  939.4 2.4 collective-permute-start
  948.3 36.7 %all-reduce.5.cloned.1.call-done = (f32[3,64,64]{2,1,0:T(8,128)}, f32[3,64,64]{2,1,0:T(8,128)}) async-done(((f32[3,64,64]{2,1,0:T(8,128)}, f32[3,64,64]{2,1,0:T(8,128)}), (f32[3,64,64]{2,1,0:T(8,128)}, f32[3,64,64]{2,1,0:T(8,128)})) %all-reduce.5.cloned.1.call-update) | async-done | bytes 98320 | tf_op jit(solution)/shard_map/while/body/eval_jaxpr/psum | solution.py:64
  986.4 77.3 %psum.43 = f32[3,1,4096]{2,0,1:T(4,128)S(1)} all-reduce(f32[3,1,4096]{2,0,1:T(4,128)S(1)} %reshape.292), channel_id=1, replica_groups=mesh['dp'=16,'pipe'=4,'tensor'=4] {'dp'}, use_global_device_ids=true, to_apply=%region_3.3 | all-reduce | flops 12288 | bytes 98304 | tf_op jit(solution)/shard_map/while/body/eval_jaxpr/psum | solution.py:85
  1068.3 1.6 select_dynamic-update-slice_fusion.2
  1069.9 2.4 collective-permute-start
  1078.9 36.7 %all-reduce.5.cloned.1.call-done = (f32[3,64,64]{2,1,0:T(8,128)}, f32[3,64,64]{2,1,0:T(8,128)}) async-done(((f32[3,64,64]{2,1,0:T(8,128)}, f32[3,64,64]{2,1,0:T(8,128)}), (f32[3,64,64]{2,1,0:T(8,128)}, f32[3,64,64]{2,1,0:T(8,128)})) %all-reduce.5.cloned.1.call-update) | async-done | bytes 98320 | tf_op jit(solution)/shard_map/while/body/eval_jaxpr/psum | solution.py:64
  1117.0 77.3 %psum.43 = f32[3,1,4096]{2,0,1:T(4,128)S(1)} all-reduce(f32[3,1,4096]{2,0,1:T(4,128)S(1)} %reshape.292), channel_id=1, replica_groups=mesh['dp'=16,'pipe'=4,'tensor'=4] {'dp'}, use_global_device_ids=true, to_apply=%region_3.3 | all-reduce | flops 12288 | bytes 98304 | tf_op jit(solution)/shard_map/while/body/eval_jaxpr/psum | solution.py:85
  1198.8 1.6 select_dynamic-update-slice_fusion.2
  1200.5 2.4 collective-permute-start
  1209.4 36.7 %all-reduce.5.cloned.1.call-done = (f32[3,64,64]{2,1,0:T(8,128)}, f32[3,64,64]{2,1,0:T(8,128)}) async-done(((f32[3,64,64]{2,1,0:T(8,128)}, f32[3,64,64]{2,1,0:T(8,128)}), (f32[3,64,64]{2,1,0:T(8,128)}, f32[3,64,64]{2,1,0:T(8,128)})) %all-reduce.5.cloned.1.call-update) | async-done | bytes 98320 | tf_op jit(solution)/shard_map/while/body/eval_jaxpr/psum | solution.py:64
  1247.5 77.3 %psum.43 = f32[3,1,4096]{2,0,1:T(4,128)S(1)} all-reduce(f32[3,1,4096]{2,0,1:T(4,128)S(1)} %reshape.292), channel_id=1, replica_groups=mesh['dp'=16,'pipe'=4,'tensor'=4] {'dp'}, use_global_device_ids=true, to_apply=%region_3.3 | all-reduce | flops 12288 | bytes 98304 | tf_op jit(solution)/shard_map/while/body/eval_jaxpr/psum | solution.py:85
  1329.4 1.6 select_dynamic-update-slice_fusion.2
  1331.0 2.4 collective-permute-start
  1339.9 36.7 %all-reduce.5.cloned.1.call-done = (f32[3,64,64]{2,1,0:T(8,128)}, f32[3,64,64]{2,1,0:T(8,128)}) async-done(((f32[3,64,64]{2,1,0:T(8,128)}, f32[3,64,64]{2,1,0:T(8,128)}), (f32[3,64,64]{2,1,0:T(8,128)}, f32[3,64,64]{2,1,0:T(8,128)})) %all-reduce.5.cloned.1.call-update) | async-done | bytes 98320 | tf_op jit(solution)/shard_map/while/body/eval_jaxpr/psum | solution.py:64
  1378.0 77.3 %psum.43 = f32[3,1,4096]{2,0,1:T(4,128)S(1)} all-reduce(f32[3,1,4096]{2,0,1:T(4,128)S(1)} %reshape.292), channel_id=1, replica_groups=mesh['dp'=16,'pipe'=4,'tensor'=4] {'dp'}, use_global_device_ids=true, to_apply=%region_3.3 | all-reduce | flops 12288 | bytes 98304 | tf_op jit(solution)/shard_map/while/body/eval_jaxpr/psum | solution.py:85
  (418 shorter events, 135.5 us)
Async XLA Ops:
  7.2 3.6 copy-start
  7.2 6.1 copy-start.1
  13.3 58.0 %all-reduce.5.cloned.1.call-start = ((), (), s32[]{:S(2)}) async-start(), calls=%async_computation | async-start | bytes 393216 | tf_op jit(solution)/shard_map/while/body/eval_jaxpr/psum | solution.py:64
  19.0 131.6 %collective-permute-start = (bf16[1,64,1024]{2,1,0:T(8,128)(2,1)S(1)}, bf16[1,64,1024]{2,1,0:T(8,128)(2,1)S(1)}, u32[]{:S(2)}, u32[]{:S(2)}) collective-permute-start(bf16[1,64,1024]{2,1,0:T(8,128)(2,1)S(1)} %get-tuple-element.449), channel_id=1, source_target_pairs={{4,0},{8,4},{12,8},{5,1},{9,5},{13,9},{6,2},{10,6},{14,10},{7,3},{... | collective-permute-start | bytes 393224 | tf_op jit(solution)/shard_map/while/body/eval_jaxpr/ppermute | solution.py:11
  150.6 51.3 %all-reduce.5.cloned.1.call-start = ((), (), s32[]{:S(2)}) async-start(), calls=%async_computation | async-start | bytes 393216 | tf_op jit(solution)/shard_map/while/body/eval_jaxpr/psum | solution.py:64
  156.3 124.8 %collective-permute-start = (bf16[1,64,1024]{2,1,0:T(8,128)(2,1)S(1)}, bf16[1,64,1024]{2,1,0:T(8,128)(2,1)S(1)}, u32[]{:S(2)}, u32[]{:S(2)}) collective-permute-start(bf16[1,64,1024]{2,1,0:T(8,128)(2,1)S(1)} %get-tuple-element.449), channel_id=1, source_target_pairs={{4,0},{8,4},{12,8},{5,1},{9,5},{13,9},{6,2},{10,6},{14,10},{7,3},{... | collective-permute-start | bytes 393224 | tf_op jit(solution)/shard_map/while/body/eval_jaxpr/ppermute | solution.py:11
  281.1 51.3 %all-reduce.5.cloned.1.call-start = ((), (), s32[]{:S(2)}) async-start(), calls=%async_computation | async-start | bytes 393216 | tf_op jit(solution)/shard_map/while/body/eval_jaxpr/psum | solution.py:64
  286.8 124.8 %collective-permute-start = (bf16[1,64,1024]{2,1,0:T(8,128)(2,1)S(1)}, bf16[1,64,1024]{2,1,0:T(8,128)(2,1)S(1)}, u32[]{:S(2)}, u32[]{:S(2)}) collective-permute-start(bf16[1,64,1024]{2,1,0:T(8,128)(2,1)S(1)} %get-tuple-element.449), channel_id=1, source_target_pairs={{4,0},{8,4},{12,8},{5,1},{9,5},{13,9},{6,2},{10,6},{14,10},{7,3},{... | collective-permute-start | bytes 393224 | tf_op jit(solution)/shard_map/while/body/eval_jaxpr/ppermute | solution.py:11
  411.6 51.3 %all-reduce.5.cloned.1.call-start = ((), (), s32[]{:S(2)}) async-start(), calls=%async_computation | async-start | bytes 393216 | tf_op jit(solution)/shard_map/while/body/eval_jaxpr/psum | solution.py:64
  417.3 124.8 %collective-permute-start = (bf16[1,64,1024]{2,1,0:T(8,128)(2,1)S(1)}, bf16[1,64,1024]{2,1,0:T(8,128)(2,1)S(1)}, u32[]{:S(2)}, u32[]{:S(2)}) collective-permute-start(bf16[1,64,1024]{2,1,0:T(8,128)(2,1)S(1)} %get-tuple-element.449), channel_id=1, source_target_pairs={{4,0},{8,4},{12,8},{5,1},{9,5},{13,9},{6,2},{10,6},{14,10},{7,3},{... | collective-permute-start | bytes 393224 | tf_op jit(solution)/shard_map/while/body/eval_jaxpr/ppermute | solution.py:11
  542.1 51.3 %all-reduce.5.cloned.1.call-start = ((), (), s32[]{:S(2)}) async-start(), calls=%async_computation | async-start | bytes 393216 | tf_op jit(solution)/shard_map/while/body/eval_jaxpr/psum | solution.py:64
  547.8 124.8 %collective-permute-start = (bf16[1,64,1024]{2,1,0:T(8,128)(2,1)S(1)}, bf16[1,64,1024]{2,1,0:T(8,128)(2,1)S(1)}, u32[]{:S(2)}, u32[]{:S(2)}) collective-permute-start(bf16[1,64,1024]{2,1,0:T(8,128)(2,1)S(1)} %get-tuple-element.449), channel_id=1, source_target_pairs={{4,0},{8,4},{12,8},{5,1},{9,5},{13,9},{6,2},{10,6},{14,10},{7,3},{... | collective-permute-start | bytes 393224 | tf_op jit(solution)/shard_map/while/body/eval_jaxpr/ppermute | solution.py:11
  672.7 51.3 %all-reduce.5.cloned.1.call-start = ((), (), s32[]{:S(2)}) async-start(), calls=%async_computation | async-start | bytes 393216 | tf_op jit(solution)/shard_map/while/body/eval_jaxpr/psum | solution.py:64
  678.4 124.8 %collective-permute-start = (bf16[1,64,1024]{2,1,0:T(8,128)(2,1)S(1)}, bf16[1,64,1024]{2,1,0:T(8,128)(2,1)S(1)}, u32[]{:S(2)}, u32[]{:S(2)}) collective-permute-start(bf16[1,64,1024]{2,1,0:T(8,128)(2,1)S(1)} %get-tuple-element.449), channel_id=1, source_target_pairs={{4,0},{8,4},{12,8},{5,1},{9,5},{13,9},{6,2},{10,6},{14,10},{7,3},{... | collective-permute-start | bytes 393224 | tf_op jit(solution)/shard_map/while/body/eval_jaxpr/ppermute | solution.py:11
  803.2 51.3 %all-reduce.5.cloned.1.call-start = ((), (), s32[]{:S(2)}) async-start(), calls=%async_computation | async-start | bytes 393216 | tf_op jit(solution)/shard_map/while/body/eval_jaxpr/psum | solution.py:64
  808.9 124.8 %collective-permute-start = (bf16[1,64,1024]{2,1,0:T(8,128)(2,1)S(1)}, bf16[1,64,1024]{2,1,0:T(8,128)(2,1)S(1)}, u32[]{:S(2)}, u32[]{:S(2)}) collective-permute-start(bf16[1,64,1024]{2,1,0:T(8,128)(2,1)S(1)} %get-tuple-element.449), channel_id=1, source_target_pairs={{4,0},{8,4},{12,8},{5,1},{9,5},{13,9},{6,2},{10,6},{14,10},{7,3},{... | collective-permute-start | bytes 393224 | tf_op jit(solution)/shard_map/while/body/eval_jaxpr/ppermute | solution.py:11
  933.7 51.3 %all-reduce.5.cloned.1.call-start = ((), (), s32[]{:S(2)}) async-start(), calls=%async_computation | async-start | bytes 393216 | tf_op jit(solution)/shard_map/while/body/eval_jaxpr/psum | solution.py:64
  939.4 124.8 %collective-permute-start = (bf16[1,64,1024]{2,1,0:T(8,128)(2,1)S(1)}, bf16[1,64,1024]{2,1,0:T(8,128)(2,1)S(1)}, u32[]{:S(2)}, u32[]{:S(2)}) collective-permute-start(bf16[1,64,1024]{2,1,0:T(8,128)(2,1)S(1)} %get-tuple-element.449), channel_id=1, source_target_pairs={{4,0},{8,4},{12,8},{5,1},{9,5},{13,9},{6,2},{10,6},{14,10},{7,3},{... | collective-permute-start | bytes 393224 | tf_op jit(solution)/shard_map/while/body/eval_jaxpr/ppermute | solution.py:11
  1064.2 51.3 %all-reduce.5.cloned.1.call-start = ((), (), s32[]{:S(2)}) async-start(), calls=%async_computation | async-start | bytes 393216 | tf_op jit(solution)/shard_map/while/body/eval_jaxpr/psum | solution.py:64
  1069.9 124.8 %collective-permute-start = (bf16[1,64,1024]{2,1,0:T(8,128)(2,1)S(1)}, bf16[1,64,1024]{2,1,0:T(8,128)(2,1)S(1)}, u32[]{:S(2)}, u32[]{:S(2)}) collective-permute-start(bf16[1,64,1024]{2,1,0:T(8,128)(2,1)S(1)} %get-tuple-element.449), channel_id=1, source_target_pairs={{4,0},{8,4},{12,8},{5,1},{9,5},{13,9},{6,2},{10,6},{14,10},{7,3},{... | collective-permute-start | bytes 393224 | tf_op jit(solution)/shard_map/while/body/eval_jaxpr/ppermute | solution.py:11
  1194.8 51.3 %all-reduce.5.cloned.1.call-start = ((), (), s32[]{:S(2)}) async-start(), calls=%async_computation | async-start | bytes 393216 | tf_op jit(solution)/shard_map/while/body/eval_jaxpr/psum | solution.py:64
  1200.5 124.8 %collective-permute-start = (bf16[1,64,1024]{2,1,0:T(8,128)(2,1)S(1)}, bf16[1,64,1024]{2,1,0:T(8,128)(2,1)S(1)}, u32[]{:S(2)}, u32[]{:S(2)}) collective-permute-start(bf16[1,64,1024]{2,1,0:T(8,128)(2,1)S(1)} %get-tuple-element.449), channel_id=1, source_target_pairs={{4,0},{8,4},{12,8},{5,1},{9,5},{13,9},{6,2},{10,6},{14,10},{7,3},{... | collective-permute-start | bytes 393224 | tf_op jit(solution)/shard_map/while/body/eval_jaxpr/ppermute | solution.py:11
  1325.3 51.3 %all-reduce.5.cloned.1.call-start = ((), (), s32[]{:S(2)}) async-start(), calls=%async_computation | async-start | bytes 393216 | tf_op jit(solution)/shard_map/while/body/eval_jaxpr/psum | solution.py:64
  1331.0 124.8 %collective-permute-start = (bf16[1,64,1024]{2,1,0:T(8,128)(2,1)S(1)}, bf16[1,64,1024]{2,1,0:T(8,128)(2,1)S(1)}, u32[]{:S(2)}, u32[]{:S(2)}) collective-permute-start(bf16[1,64,1024]{2,1,0:T(8,128)(2,1)S(1)} %get-tuple-element.449), channel_id=1, source_target_pairs={{4,0},{8,4},{12,8},{5,1},{9,5},{13,9},{6,2},{10,6},{14,10},{7,3},{... | collective-permute-start | bytes 393224 | tf_op jit(solution)/shard_map/while/body/eval_jaxpr/ppermute | solution.py:11
  1455.8 0.7 copy-start.2
Sparse Core Ops, SparseCore 0:
  28.9 42.4 all-reduce.4
  164.6 37.2 all-reduce.4
  295.1 37.2 all-reduce.4
  425.6 37.2 all-reduce.4
  556.1 37.2 all-reduce.4
  686.7 37.2 all-reduce.4
  817.2 37.2 all-reduce.4
  947.7 37.2 all-reduce.4
  1078.2 37.2 all-reduce.4
  1208.8 37.2 all-reduce.4
  1339.3 37.2 all-reduce.4
where the time goes:
time: 1470 us; the launch traced here: 1460 us
  blocking collectives  850 us (58%)
  waiting for transfers between devices  409 us (28%)
  matrix products  77.6 us (5%)
  other arithmetic  51.4 us (3%)
  starting transfers between devices  28.8 us (2%)
  local copies, waits for them, and re-layouts  27.7 us (2%)
  between operations  15.8 us (1%)
    psum x11, blocking collectives, turn(): sketch = lax.psum(sketch, 'dp')  850 us
    psum x11, waiting for transfers between devices, process(): lax.psum((jnp.stack(act_parts), jnp.stack(delta_parts)), 'tensor')  409 us
    dot_general x33, matrix products, process(): jnp.dot(flat_act, dense[slot, :, :rank], preferred_element_type=jnp.float32)  35.7 us
  transfers between devices with their start and end apart: 22, of which 11 were waited for; matrix products, arithmetic and copies ran while one was open for 6% of the time, Pallas kernels for 0%

commit v1 on v0

--- a/solution.py
+++ b/solution.py
@@ -82,7 +82,7 @@
         top = lax.dynamic_slice_in_dim(grad_out, start, width, 0)
         grad = jnp.where(segment == segments - 1, top, incoming)
         grad, sketch = process(grad, start, width)
-        sketch = lax.psum(sketch, "dp")
+        sketch = jnp.sum(lax.all_gather(sketch, axis_name="dp"), axis=0)
         old_out = lax.dynamic_slice_in_dim(segment_out, start, width, 0)
         segment_out = lax.dynamic_update_slice_in_dim(
             segment_out, jnp.where(valid, grad, old_out), start, 0

time: 1470 us -> 1150 us (0.78)
  blocking collectives: 850 us -> 503 us
  other arithmetic: 51.4 us -> 69.6 us
  local copies, waits for them, and re-layouts: 27.7 us -> 42.5 us
    psum x11 -> x0, blocking collectives: 850 us -> none  [turn(): sketch = lax.psum(sketch, 'dp')]
    all_gather x0 -> x11, blocking collectives: none -> 503 us  [turn(): sketch = jnp.sum(lax.all_gather(sketch, axis_name='dp'), axis=0)]
    dynamic_update_slice x22 -> x11, local copies, waits for them, and re-layouts: 4.96 us -> 20.2 us  [turn(): lax.dynamic_update_slice_in_dim(sketches, jnp.where(valid, sketch, old_sk...]
  transfers between devices with their start and end apart: 22 -> 22, of which waited for: 11 -> 11; matrix products, arithmetic and copies ran while one was open for 6% -> 11% of each run, Pallas kernels for 0% -> 0%
where the time goes in v1:
time: 1150 us
  blocking collectives  503 us (44%)
  waiting for transfers between devices  411 us (36%)
  matrix products  77.6 us (7%)
  other arithmetic  69.6 us (6%)
  local copies, waits for them, and re-layouts  42.5 us (4%)
  starting transfers between devices  28.4 us (2%)
  between operations  15.7 us (1%)
    all_gather x11, blocking collectives, turn(): sketch = jnp.sum(lax.all_gather(sketch, axis_name='dp'), axis=0)  503 us
    psum x11, waiting for transfers between devices, process(): lax.psum((jnp.stack(act_parts), jnp.stack(delta_parts)), 'tensor')  411 us
    dot_general x33, matrix products, process(): jnp.dot(flat_act, dense[slot, :, :rank], preferred_element_type=jnp.float32)  35.7 us
    ppermute x11, starting transfers between devices, shifted(): return lax.ppermute(x, axis, pairs)  28.4 us
  transfers between devices with their start and end apart: 22, of which 11 were waited for; matrix products, arithmetic and copies ran while one was open for 11% of the time, Pallas kernels for 0%

profile of v1, /device:TPU:8, one launch (start us, length us, event | category | flops | bytes accessed | tf_op | source)
XLA Modules:
  0.0 1150.0 jit_solution(5238791477257663822)
XLA Ops:
  13.9 1129.6 %while.20 = (s32[]{:T(128)}, bf16[1,64,1024]{2,1,0:T(8,128)(2,1)S(1)}, bf16[8,64,1024]{2,1,0:T(8,128)(2,1)}, f32[3,8,4096]{2,1,0:T(8,128)}, pred[]{:T(512)}, /*i...) while((s32[]{:T(128)}, ...), condition=%wide.region_4.5_spmd.clone, body=%wide.region_0.4_spmd.clone.sunk | while | flops 163479552 | bytes 17400736 | solution.py:102
  19.5 4.1 collective-permute-start
  30.0 42.0 %all-reduce.5.cloned.1.call-done = (f32[3,64,64]{2,1,0:T(8,128)}, f32[3,64,64]{2,1,0:T(8,128)}) async-done(((f32[3,64,64]{2,1,0:T(8,128)}, f32[3,64,64]{2,1,0:T(8,128)}), (f32[3,64,64]{2,1,0:T(8,128)}, f32[3,64,64]{2,1,0:T(8,128)})) %all-reduce.5.cloned.1.call-update) | async-done | bytes 98320 | tf_op jit(solution)/shard_map/while/body/eval_jaxpr/psum | solution.py:64
  73.3 45.7 %all_gather.11 = f32[16,3,1,4096]{3,2,1,0:T(1,128)S(1)} all-gather(f32[1,3,1,4096]{3,2,1,0:T(1,128)S(1)} %reshape.298), channel_id=1, replica_groups=mesh['dp'=16,'pipe'=4,'tensor'=4] {'dp'}, dimensions={0}, use_global_device_ids=true | all-gather | bytes 835584 | tf_op jit(solution)/shard_map/while/body/eval_jaxpr/all_gather | solution.py:85
  120.8 1.8 dynamic_update_slice.24
  126.7 1.6 select_dynamic-update-slice_fusion.2
  128.3 2.4 collective-permute-start
  137.1 36.9 %all-reduce.5.cloned.1.call-done = (f32[3,64,64]{2,1,0:T(8,128)}, f32[3,64,64]{2,1,0:T(8,128)}) async-done(((f32[3,64,64]{2,1,0:T(8,128)}, f32[3,64,64]{2,1,0:T(8,128)}), (f32[3,64,64]{2,1,0:T(8,128)}, f32[3,64,64]{2,1,0:T(8,128)})) %all-reduce.5.cloned.1.call-update) | async-done | bytes 98320 | tf_op jit(solution)/shard_map/while/body/eval_jaxpr/psum | solution.py:64
  175.4 45.7 %all_gather.11 = f32[16,3,1,4096]{3,2,1,0:T(1,128)S(1)} all-gather(f32[1,3,1,4096]{3,2,1,0:T(1,128)S(1)} %reshape.298), channel_id=1, replica_groups=mesh['dp'=16,'pipe'=4,'tensor'=4] {'dp'}, dimensions={0}, use_global_device_ids=true | all-gather | bytes 835584 | tf_op jit(solution)/shard_map/while/body/eval_jaxpr/all_gather | solution.py:85
  222.9 1.8 dynamic_update_slice.24
  228.8 1.6 select_dynamic-update-slice_fusion.2
  230.4 2.4 collective-permute-start
  239.2 36.9 %all-reduce.5.cloned.1.call-done = (f32[3,64,64]{2,1,0:T(8,128)}, f32[3,64,64]{2,1,0:T(8,128)}) async-done(((f32[3,64,64]{2,1,0:T(8,128)}, f32[3,64,64]{2,1,0:T(8,128)}), (f32[3,64,64]{2,1,0:T(8,128)}, f32[3,64,64]{2,1,0:T(8,128)})) %all-reduce.5.cloned.1.call-update) | async-done | bytes 98320 | tf_op jit(solution)/shard_map/while/body/eval_jaxpr/psum | solution.py:64
  277.5 45.7 %all_gather.11 = f32[16,3,1,4096]{3,2,1,0:T(1,128)S(1)} all-gather(f32[1,3,1,4096]{3,2,1,0:T(1,128)S(1)} %reshape.298), channel_id=1, replica_groups=mesh['dp'=16,'pipe'=4,'tensor'=4] {'dp'}, dimensions={0}, use_global_device_ids=true | all-gather | bytes 835584 | tf_op jit(solution)/shard_map/while/body/eval_jaxpr/all_gather | solution.py:85
  325.0 1.8 dynamic_update_slice.24
  332.5 2.4 collective-permute-start
  341.3 36.9 %all-reduce.5.cloned.1.call-done = (f32[3,64,64]{2,1,0:T(8,128)}, f32[3,64,64]{2,1,0:T(8,128)}) async-done(((f32[3,64,64]{2,1,0:T(8,128)}, f32[3,64,64]{2,1,0:T(8,128)}), (f32[3,64,64]{2,1,0:T(8,128)}, f32[3,64,64]{2,1,0:T(8,128)})) %all-reduce.5.cloned.1.call-update) | async-done | bytes 98320 | tf_op jit(solution)/shard_map/while/body/eval_jaxpr/psum | solution.py:64
  379.6 45.7 %all_gather.11 = f32[16,3,1,4096]{3,2,1,0:T(1,128)S(1)} all-gather(f32[1,3,1,4096]{3,2,1,0:T(1,128)S(1)} %reshape.298), channel_id=1, replica_groups=mesh['dp'=16,'pipe'=4,'tensor'=4] {'dp'}, dimensions={0}, use_global_device_ids=true | all-gather | bytes 835584 | tf_op jit(solution)/shard_map/while/body/eval_jaxpr/all_gather | solution.py:85
  427.1 1.8 dynamic_update_slice.24
  432.9 1.6 select_dynamic-update-slice_fusion.2
  434.5 2.4 collective-permute-start
  443.4 36.9 %all-reduce.5.cloned.1.call-done = (f32[3,64,64]{2,1,0:T(8,128)}, f32[3,64,64]{2,1,0:T(8,128)}) async-done(((f32[3,64,64]{2,1,0:T(8,128)}, f32[3,64,64]{2,1,0:T(8,128)}), (f32[3,64,64]{2,1,0:T(8,128)}, f32[3,64,64]{2,1,0:T(8,128)})) %all-reduce.5.cloned.1.call-update) | async-done | bytes 98320 | tf_op jit(solution)/shard_map/while/body/eval_jaxpr/psum | solution.py:64
  481.7 45.7 %all_gather.11 = f32[16,3,1,4096]{3,2,1,0:T(1,128)S(1)} all-gather(f32[1,3,1,4096]{3,2,1,0:T(1,128)S(1)} %reshape.298), channel_id=1, replica_groups=mesh['dp'=16,'pipe'=4,'tensor'=4] {'dp'}, dimensions={0}, use_global_device_ids=true | all-gather | bytes 835584 | tf_op jit(solution)/shard_map/while/body/eval_jaxpr/all_gather | solution.py:85
  529.1 1.8 dynamic_update_slice.24
  536.6 2.4 collective-permute-start
  545.4 36.9 %all-reduce.5.cloned.1.call-done = (f32[3,64,64]{2,1,0:T(8,128)}, f32[3,64,64]{2,1,0:T(8,128)}) async-done(((f32[3,64,64]{2,1,0:T(8,128)}, f32[3,64,64]{2,1,0:T(8,128)}), (f32[3,64,64]{2,1,0:T(8,128)}, f32[3,64,64]{2,1,0:T(8,128)})) %all-reduce.5.cloned.1.call-update) | async-done | bytes 98320 | tf_op jit(solution)/shard_map/while/body/eval_jaxpr/psum | solution.py:64
  583.7 45.7 %all_gather.11 = f32[16,3,1,4096]{3,2,1,0:T(1,128)S(1)} all-gather(f32[1,3,1,4096]{3,2,1,0:T(1,128)S(1)} %reshape.298), channel_id=1, replica_groups=mesh['dp'=16,'pipe'=4,'tensor'=4] {'dp'}, dimensions={0}, use_global_device_ids=true | all-gather | bytes 835584 | tf_op jit(solution)/shard_map/while/body/eval_jaxpr/all_gather | solution.py:85
  631.2 1.8 dynamic_update_slice.24
  638.7 2.4 collective-permute-start
  647.5 36.9 %all-reduce.5.cloned.1.call-done = (f32[3,64,64]{2,1,0:T(8,128)}, f32[3,64,64]{2,1,0:T(8,128)}) async-done(((f32[3,64,64]{2,1,0:T(8,128)}, f32[3,64,64]{2,1,0:T(8,128)}), (f32[3,64,64]{2,1,0:T(8,128)}, f32[3,64,64]{2,1,0:T(8,128)})) %all-reduce.5.cloned.1.call-update) | async-done | bytes 98320 | tf_op jit(solution)/shard_map/while/body/eval_jaxpr/psum | solution.py:64
  685.8 45.7 %all_gather.11 = f32[16,3,1,4096]{3,2,1,0:T(1,128)S(1)} all-gather(f32[1,3,1,4096]{3,2,1,0:T(1,128)S(1)} %reshape.298), channel_id=1, replica_groups=mesh['dp'=16,'pipe'=4,'tensor'=4] {'dp'}, dimensions={0}, use_global_device_ids=true | all-gather | bytes 835584 | tf_op jit(solution)/shard_map/while/body/eval_jaxpr/all_gather | solution.py:85
  733.3 1.8 dynamic_update_slice.24
  740.8 2.4 collective-permute-start
  749.6 36.9 %all-reduce.5.cloned.1.call-done = (f32[3,64,64]{2,1,0:T(8,128)}, f32[3,64,64]{2,1,0:T(8,128)}) async-done(((f32[3,64,64]{2,1,0:T(8,128)}, f32[3,64,64]{2,1,0:T(8,128)}), (f32[3,64,64]{2,1,0:T(8,128)}, f32[3,64,64]{2,1,0:T(8,128)})) %all-reduce.5.cloned.1.call-update) | async-done | bytes 98320 | tf_op jit(solution)/shard_map/while/body/eval_jaxpr/psum | solution.py:64
  787.9 45.7 %all_gather.11 = f32[16,3,1,4096]{3,2,1,0:T(1,128)S(1)} all-gather(f32[1,3,1,4096]{3,2,1,0:T(1,128)S(1)} %reshape.298), channel_id=1, replica_groups=mesh['dp'=16,'pipe'=4,'tensor'=4] {'dp'}, dimensions={0}, use_global_device_ids=true | all-gather | bytes 835584 | tf_op jit(solution)/shard_map/while/body/eval_jaxpr/all_gather | solution.py:85
  835.4 1.8 dynamic_update_slice.24
  842.9 2.4 collective-permute-start
  851.7 36.9 %all-reduce.5.cloned.1.call-done = (f32[3,64,64]{2,1,0:T(8,128)}, f32[3,64,64]{2,1,0:T(8,128)}) async-done(((f32[3,64,64]{2,1,0:T(8,128)}, f32[3,64,64]{2,1,0:T(8,128)}), (f32[3,64,64]{2,1,0:T(8,128)}, f32[3,64,64]{2,1,0:T(8,128)})) %all-reduce.5.cloned.1.call-update) | async-done | bytes 98320 | tf_op jit(solution)/shard_map/while/body/eval_jaxpr/psum | solution.py:64
  890.0 45.7 %all_gather.11 = f32[16,3,1,4096]{3,2,1,0:T(1,128)S(1)} all-gather(f32[1,3,1,4096]{3,2,1,0:T(1,128)S(1)} %reshape.298), channel_id=1, replica_groups=mesh['dp'=16,'pipe'=4,'tensor'=4] {'dp'}, dimensions={0}, use_global_device_ids=true | all-gather | bytes 835584 | tf_op jit(solution)/shard_map/while/body/eval_jaxpr/all_gather | solution.py:85
  937.5 1.8 dynamic_update_slice.24
  944.9 2.4 collective-permute-start
  953.8 36.9 %all-reduce.5.cloned.1.call-done = (f32[3,64,64]{2,1,0:T(8,128)}, f32[3,64,64]{2,1,0:T(8,128)}) async-done(((f32[3,64,64]{2,1,0:T(8,128)}, f32[3,64,64]{2,1,0:T(8,128)}), (f32[3,64,64]{2,1,0:T(8,128)}, f32[3,64,64]{2,1,0:T(8,128)})) %all-reduce.5.cloned.1.call-update) | async-done | bytes 98320 | tf_op jit(solution)/shard_map/while/body/eval_jaxpr/psum | solution.py:64
  992.0 45.7 %all_gather.11 = f32[16,3,1,4096]{3,2,1,0:T(1,128)S(1)} all-gather(f32[1,3,1,4096]{3,2,1,0:T(1,128)S(1)} %reshape.298), channel_id=1, replica_groups=mesh['dp'=16,'pipe'=4,'tensor'=4] {'dp'}, dimensions={0}, use_global_device_ids=true | all-gather | bytes 835584 | tf_op jit(solution)/shard_map/while/body/eval_jaxpr/all_gather | solution.py:85
  1039.5 1.8 dynamic_update_slice.24
  1047.0 2.4 collective-permute-start
  1055.8 36.9 %all-reduce.5.cloned.1.call-done = (f32[3,64,64]{2,1,0:T(8,128)}, f32[3,64,64]{2,1,0:T(8,128)}) async-done(((f32[3,64,64]{2,1,0:T(8,128)}, f32[3,64,64]{2,1,0:T(8,128)}), (f32[3,64,64]{2,1,0:T(8,128)}, f32[3,64,64]{2,1,0:T(8,128)})) %all-reduce.5.cloned.1.call-update) | async-done | bytes 98320 | tf_op jit(solution)/shard_map/while/body/eval_jaxpr/psum | solution.py:64
  1094.1 45.7 %all_gather.11 = f32[16,3,1,4096]{3,2,1,0:T(1,128)S(1)} all-gather(f32[1,3,1,4096]{3,2,1,0:T(1,128)S(1)} %reshape.298), channel_id=1, replica_groups=mesh['dp'=16,'pipe'=4,'tensor'=4] {'dp'}, dimensions={0}, use_global_device_ids=true | all-gather | bytes 835584 | tf_op jit(solution)/shard_map/while/body/eval_jaxpr/all_gather | solution.py:85
  1141.6 1.8 dynamic_update_slice.24
  (405 shorter events, 164.9 us)
Async XLA Ops:
  7.2 3.4 copy-start
  7.2 6.7 copy-start.1
  13.9 58.0 %all-reduce.5.cloned.1.call-start = ((), (), s32[]{:S(2)}) async-start(), calls=%async_computation | async-start | bytes 393216 | tf_op jit(solution)/shard_map/while/body/eval_jaxpr/psum | solution.py:64
  19.5 103.1 %collective-permute-start = (bf16[1,64,1024]{2,1,0:T(8,128)(2,1)S(1)}, bf16[1,64,1024]{2,1,0:T(8,128)(2,1)S(1)}, u32[]{:S(2)}, u32[]{:S(2)}) collective-permute-start(bf16[1,64,1024]{2,1,0:T(8,128)(2,1)S(1)} %get-tuple-element.449), channel_id=1, source_target_pairs={{4,0},{8,4},{12,8},{5,1},{9,5},{13,9},{6,2},{10,6},{14,10},{7,3},{... | collective-permute-start | bytes 393224 | tf_op jit(solution)/shard_map/while/body/eval_jaxpr/ppermute | solution.py:11
  122.7 51.4 %all-reduce.5.cloned.1.call-start = ((), (), s32[]{:S(2)}) async-start(), calls=%async_computation | async-start | bytes 393216 | tf_op jit(solution)/shard_map/while/body/eval_jaxpr/psum | solution.py:64
  128.3 96.5 %collective-permute-start = (bf16[1,64,1024]{2,1,0:T(8,128)(2,1)S(1)}, bf16[1,64,1024]{2,1,0:T(8,128)(2,1)S(1)}, u32[]{:S(2)}, u32[]{:S(2)}) collective-permute-start(bf16[1,64,1024]{2,1,0:T(8,128)(2,1)S(1)} %get-tuple-element.449), channel_id=1, source_target_pairs={{4,0},{8,4},{12,8},{5,1},{9,5},{13,9},{6,2},{10,6},{14,10},{7,3},{... | collective-permute-start | bytes 393224 | tf_op jit(solution)/shard_map/while/body/eval_jaxpr/ppermute | solution.py:11
  224.8 51.3 %all-reduce.5.cloned.1.call-start = ((), (), s32[]{:S(2)}) async-start(), calls=%async_computation | async-start | bytes 393216 | tf_op jit(solution)/shard_map/while/body/eval_jaxpr/psum | solution.py:64
  230.4 96.4 %collective-permute-start = (bf16[1,64,1024]{2,1,0:T(8,128)(2,1)S(1)}, bf16[1,64,1024]{2,1,0:T(8,128)(2,1)S(1)}, u32[]{:S(2)}, u32[]{:S(2)}) collective-permute-start(bf16[1,64,1024]{2,1,0:T(8,128)(2,1)S(1)} %get-tuple-element.449), channel_id=1, source_target_pairs={{4,0},{8,4},{12,8},{5,1},{9,5},{13,9},{6,2},{10,6},{14,10},{7,3},{... | collective-permute-start | bytes 393224 | tf_op jit(solution)/shard_map/while/body/eval_jaxpr/ppermute | solution.py:11
  326.8 51.3 %all-reduce.5.cloned.1.call-start = ((), (), s32[]{:S(2)}) async-start(), calls=%async_computation | async-start | bytes 393216 | tf_op jit(solution)/shard_map/while/body/eval_jaxpr/psum | solution.py:64
  332.5 96.4 %collective-permute-start = (bf16[1,64,1024]{2,1,0:T(8,128)(2,1)S(1)}, bf16[1,64,1024]{2,1,0:T(8,128)(2,1)S(1)}, u32[]{:S(2)}, u32[]{:S(2)}) collective-permute-start(bf16[1,64,1024]{2,1,0:T(8,128)(2,1)S(1)} %get-tuple-element.449), channel_id=1, source_target_pairs={{4,0},{8,4},{12,8},{5,1},{9,5},{13,9},{6,2},{10,6},{14,10},{7,3},{... | collective-permute-start | bytes 393224 | tf_op jit(solution)/shard_map/while/body/eval_jaxpr/ppermute | solution.py:11
  428.9 51.3 %all-reduce.5.cloned.1.call-start = ((), (), s32[]{:S(2)}) async-start(), calls=%async_computation | async-start | bytes 393216 | tf_op jit(solution)/shard_map/while/body/eval_jaxpr/psum | solution.py:64
  434.5 96.4 %collective-permute-start = (bf16[1,64,1024]{2,1,0:T(8,128)(2,1)S(1)}, bf16[1,64,1024]{2,1,0:T(8,128)(2,1)S(1)}, u32[]{:S(2)}, u32[]{:S(2)}) collective-permute-start(bf16[1,64,1024]{2,1,0:T(8,128)(2,1)S(1)} %get-tuple-element.449), channel_id=1, source_target_pairs={{4,0},{8,4},{12,8},{5,1},{9,5},{13,9},{6,2},{10,6},{14,10},{7,3},{... | collective-permute-start | bytes 393224 | tf_op jit(solution)/shard_map/while/body/eval_jaxpr/ppermute | solution.py:11
  531.0 51.3 %all-reduce.5.cloned.1.call-start = ((), (), s32[]{:S(2)}) async-start(), calls=%async_computation | async-start | bytes 393216 | tf_op jit(solution)/shard_map/while/body/eval_jaxpr/psum | solution.py:64
  536.6 96.4 %collective-permute-start = (bf16[1,64,1024]{2,1,0:T(8,128)(2,1)S(1)}, bf16[1,64,1024]{2,1,0:T(8,128)(2,1)S(1)}, u32[]{:S(2)}, u32[]{:S(2)}) collective-permute-start(bf16[1,64,1024]{2,1,0:T(8,128)(2,1)S(1)} %get-tuple-element.449), channel_id=1, source_target_pairs={{4,0},{8,4},{12,8},{5,1},{9,5},{13,9},{6,2},{10,6},{14,10},{7,3},{... | collective-permute-start | bytes 393224 | tf_op jit(solution)/shard_map/while/body/eval_jaxpr/ppermute | solution.py:11
  633.1 51.3 %all-reduce.5.cloned.1.call-start = ((), (), s32[]{:S(2)}) async-start(), calls=%async_computation | async-start | bytes 393216 | tf_op jit(solution)/shard_map/while/body/eval_jaxpr/psum | solution.py:64
  638.7 96.4 %collective-permute-start = (bf16[1,64,1024]{2,1,0:T(8,128)(2,1)S(1)}, bf16[1,64,1024]{2,1,0:T(8,128)(2,1)S(1)}, u32[]{:S(2)}, u32[]{:S(2)}) collective-permute-start(bf16[1,64,1024]{2,1,0:T(8,128)(2,1)S(1)} %get-tuple-element.449), channel_id=1, source_target_pairs={{4,0},{8,4},{12,8},{5,1},{9,5},{13,9},{6,2},{10,6},{14,10},{7,3},{... | collective-permute-start | bytes 393224 | tf_op jit(solution)/shard_map/while/body/eval_jaxpr/ppermute | solution.py:11
  735.1 51.3 %all-reduce.5.cloned.1.call-start = ((), (), s32[]{:S(2)}) async-start(), calls=%async_computation | async-start | bytes 393216 | tf_op jit(solution)/shard_map/while/body/eval_jaxpr/psum | solution.py:64
  740.8 96.4 %collective-permute-start = (bf16[1,64,1024]{2,1,0:T(8,128)(2,1)S(1)}, bf16[1,64,1024]{2,1,0:T(8,128)(2,1)S(1)}, u32[]{:S(2)}, u32[]{:S(2)}) collective-permute-start(bf16[1,64,1024]{2,1,0:T(8,128)(2,1)S(1)} %get-tuple-element.449), channel_id=1, source_target_pairs={{4,0},{8,4},{12,8},{5,1},{9,5},{13,9},{6,2},{10,6},{14,10},{7,3},{... | collective-permute-start | bytes 393224 | tf_op jit(solution)/shard_map/while/body/eval_jaxpr/ppermute | solution.py:11
  837.2 51.3 %all-reduce.5.cloned.1.call-start = ((), (), s32[]{:S(2)}) async-start(), calls=%async_computation | async-start | bytes 393216 | tf_op jit(solution)/shard_map/while/body/eval_jaxpr/psum | solution.py:64
  842.9 96.4 %collective-permute-start = (bf16[1,64,1024]{2,1,0:T(8,128)(2,1)S(1)}, bf16[1,64,1024]{2,1,0:T(8,128)(2,1)S(1)}, u32[]{:S(2)}, u32[]{:S(2)}) collective-permute-start(bf16[1,64,1024]{2,1,0:T(8,128)(2,1)S(1)} %get-tuple-element.449), channel_id=1, source_target_pairs={{4,0},{8,4},{12,8},{5,1},{9,5},{13,9},{6,2},{10,6},{14,10},{7,3},{... | collective-permute-start | bytes 393224 | tf_op jit(solution)/shard_map/while/body/eval_jaxpr/ppermute | solution.py:11
  939.3 51.3 %all-reduce.5.cloned.1.call-start = ((), (), s32[]{:S(2)}) async-start(), calls=%async_computation | async-start | bytes 393216 | tf_op jit(solution)/shard_map/while/body/eval_jaxpr/psum | solution.py:64
  944.9 96.4 %collective-permute-start = (bf16[1,64,1024]{2,1,0:T(8,128)(2,1)S(1)}, bf16[1,64,1024]{2,1,0:T(8,128)(2,1)S(1)}, u32[]{:S(2)}, u32[]{:S(2)}) collective-permute-start(bf16[1,64,1024]{2,1,0:T(8,128)(2,1)S(1)} %get-tuple-element.449), channel_id=1, source_target_pairs={{4,0},{8,4},{12,8},{5,1},{9,5},{13,9},{6,2},{10,6},{14,10},{7,3},{... | collective-permute-start | bytes 393224 | tf_op jit(solution)/shard_map/while/body/eval_jaxpr/ppermute | solution.py:11
  1041.4 51.3 %all-reduce.5.cloned.1.call-start = ((), (), s32[]{:S(2)}) async-start(), calls=%async_computation | async-start | bytes 393216 | tf_op jit(solution)/shard_map/while/body/eval_jaxpr/psum | solution.py:64
  1047.0 96.4 %collective-permute-start = (bf16[1,64,1024]{2,1,0:T(8,128)(2,1)S(1)}, bf16[1,64,1024]{2,1,0:T(8,128)(2,1)S(1)}, u32[]{:S(2)}, u32[]{:S(2)}) collective-permute-start(bf16[1,64,1024]{2,1,0:T(8,128)(2,1)S(1)} %get-tuple-element.449), channel_id=1, source_target_pairs={{4,0},{8,4},{12,8},{5,1},{9,5},{13,9},{6,2},{10,6},{14,10},{7,3},{... | collective-permute-start | bytes 393224 | tf_op jit(solution)/shard_map/while/body/eval_jaxpr/ppermute | solution.py:11
Sparse Core Ops, SparseCore 0:
  29.5 42.4 all-reduce.4
  136.6 37.3 all-reduce.4
  238.7 37.3 all-reduce.4
  340.8 37.3 all-reduce.4
  442.8 37.3 all-reduce.4
  544.9 37.3 all-reduce.4
  647.0 37.3 all-reduce.4
  749.1 37.3 all-reduce.4
  851.2 37.3 all-reduce.4
  953.2 37.3 all-reduce.4
  1055.3 37.3 all-reduce.4
